TPU v7x, 1024 devices: a whole 8x8x8 slice. The times are simulated.
1024 devices in a mesh: ctx: 32 (over y, z_hi, core), tp: 8 (over x), dp: 4 (over z_lo).
Axes of the slice: x: 8, y: 8, z: 8 (z_hi: 2, z_lo: 4; z = z_hi * 4 + z_lo), core: 2. Of those that a mesh axis runs over, the one named last changes fastest.
Arguments:
- out_grad: bfloat16 [4, 4096, 4096], P('dp', ('ctx', 'tp')), may hold values from -6 to 6
- gate_in: bfloat16 [4, 4096, 4096], P('dp', 'tp', 'ctx'), may hold values from -6 to 6
- conv_in: bfloat16 [4, 4096, 4096], P('dp', 'tp', 'ctx'), may hold values from -6 to 6
- filter_raw: float32 [4096, 4096], P(('tp', 'ctx')), may hold values from -6 to 6
- out_weight: bfloat16 [4096, 4096], P('tp'), may hold values from -0.09375 to 0.09375
Outputs:
- gate_grad_out: bfloat16 [4, 4096, 4096], P('dp', 'tp', 'ctx')
- conv_grad_out: bfloat16 [4, 4096, 4096], P('dp', 'tp', 'ctx')
- filter_grad_out: float32 [4096, 4096], P(('tp', 'ctx', 'dp'))
All inputs are finite; a program needn't handle non-finite values.
Results may differ from a plain program's by a relative error of at most 0.0049.
Values may be sent and summed in bfloat16 or wider, within the bound.
A program may use at most 32 MiB of HBM per device.

v0:
```python
import math

import jax
import jax.numpy as jnp
from jax import lax
from jax.sharding import PartitionSpec as P


def from_everyone(array, axis):
    copies = jnp.broadcast_to(array, (lax.axis_size(axis), *array.shape))
    return lax.all_to_all(copies, axis, split_axis=0, concat_axis=0, tiled=True)


def laid_out(pieces, dim):
    pieces = jnp.moveaxis(pieces, 0, dim)
    shape = pieces.shape
    return pieces.reshape(*shape[:dim], shape[dim] * shape[dim + 1], *shape[dim + 2 :])


def collect(array, axis, dim):
    pieces = from_everyone(array, axis)
    return laid_out(pieces, dim)


def split_up(array, dim, peers):
    shape = array.shape
    pieces = array.reshape(*shape[:dim], peers, shape[dim] // peers, *shape[dim + 1 :])
    return jnp.moveaxis(pieces, dim, 0)


def sent_and_summed(array, axis, dim):
    peers = lax.axis_size(axis)
    pieces = lax.all_to_all(split_up(array, dim, peers), axis, 0, 0, tiled=True)
    return jnp.sum(pieces, axis=0)


def wave_table(rows, cols, length, sign):
    product = (
        jnp.arange(rows, dtype=jnp.int32)[:, None]
        * jnp.arange(cols, dtype=jnp.int32)[None, :]
        % length
    )
    angle = product.astype(jnp.float32) * (2.0 * math.pi / length)
    return (jnp.cos(angle), sign * jnp.sin(angle))


def mix_einsum(form, left, right):
    return jnp.einsum(form, left, right, precision=lax.Precision.HIGHEST)


def forward_spectrum(signal):
    chans, length = signal.shape
    total_len = 2 * length
    bits = total_len.bit_length() - 1
    outer_len = 2 ** (bits // 2)
    inner_len = total_len // outer_len
    half_outer = outer_len // 2
    folded = signal.reshape(chans, half_outer, inner_len)
    first_re, first_im = wave_table(outer_len, half_outer, outer_len, -1.0)
    mid_re = mix_einsum("kn,cna->cka", first_re, folded)
    mid_im = mix_einsum("kn,cna->cka", first_im, folded)
    twist_re, twist_im = wave_table(outer_len, inner_len, total_len, -1.0)
    rot_re = mid_re * twist_re - mid_im * twist_im
    rot_im = mid_re * twist_im + mid_im * twist_re
    last_re, last_im = wave_table(inner_len, inner_len, inner_len, -1.0)
    out_re = mix_einsum("cka,aj->ckj", rot_re, last_re) - mix_einsum("cka,aj->ckj", rot_im, last_im)
    out_im = mix_einsum("cka,aj->ckj", rot_re, last_im) + mix_einsum("cka,aj->ckj", rot_im, last_re)
    return (out_re, out_im)


def inverse_signal(spec_re, spec_im):
    chans, outer_len, inner_len = spec_re.shape
    total_len = outer_len * inner_len
    last_re, last_im = wave_table(inner_len, inner_len, inner_len, 1.0)
    mid_re = mix_einsum("ckj,ja->cka", spec_re, last_re) - mix_einsum(
        "ckj,ja->cka", spec_im, last_im
    )
    mid_im = mix_einsum("ckj,ja->cka", spec_re, last_im) + mix_einsum(
        "ckj,ja->cka", spec_im, last_re
    )
    twist_re, twist_im = wave_table(outer_len, inner_len, total_len, 1.0)
    rot_re = mid_re * twist_re - mid_im * twist_im
    rot_im = mid_re * twist_im + mid_im * twist_re
    first_re, first_im = wave_table(outer_len // 2, outer_len, outer_len, 1.0)
    signal = mix_einsum("nk,cka->cna", first_re, rot_re) - mix_einsum(
        "nk,cka->cna", first_im, rot_im
    )
    return signal.reshape(chans, -1) / total_len


def on_device(out_grad, gate_in, conv_in, filter_raw, out_weight):
    grad_rows = out_grad[0]
    gate_local = gate_in[0]
    conv_local = conv_in[0]
    unit_grad = lax.dot_general(
        out_weight,
        collect(grad_rows, "tp", 0),
        (((1,), (1,)), ((), ())),
        preferred_element_type=jnp.float32,
    )
    gate_grad = (unit_grad * gate_local.astype(jnp.float32)).astype(jnp.bfloat16)
    gate_chan, conv_chan = (
        lax.all_to_all(gate_grad, "ctx", split_axis=0, concat_axis=1, tiled=True),
        lax.all_to_all(conv_local, "ctx", split_axis=0, concat_axis=1, tiled=True),
    )
    length = filter_raw.shape[1]
    norm_scale = 1.0 / math.sqrt(length)
    filt_re, filt_im = forward_spectrum(filter_raw * norm_scale)
    conv_re, conv_im = forward_spectrum(conv_chan.astype(jnp.float32))
    gate_re, gate_im = forward_spectrum(gate_chan.astype(jnp.float32))
    conv_out = inverse_signal(
        filt_re * conv_re - filt_im * conv_im, filt_re * conv_im + filt_im * conv_re
    ).astype(jnp.bfloat16)
    conv_grad = inverse_signal(
        filt_re * gate_re + filt_im * gate_im, filt_re * gate_im - filt_im * gate_re
    ).astype(jnp.bfloat16)
    cross_re = gate_re * conv_re + gate_im * conv_im
    cross_im = gate_im * conv_re - gate_re * conv_im
    back_out, back_grad = (
        lax.all_to_all(conv_out, "ctx", split_axis=1, concat_axis=0, tiled=True),
        lax.all_to_all(conv_grad, "ctx", split_axis=1, concat_axis=0, tiled=True),
    )
    gate_out = (unit_grad * back_out.astype(jnp.float32)).astype(jnp.bfloat16)
    filter_grad = sent_and_summed(inverse_signal(cross_re, cross_im) * norm_scale, "dp", 0)
    return (gate_out[None], back_grad[None], filter_grad)


def solution(mesh):
    placed = (
        P("dp", ("ctx", "tp"), None),
        P("dp", "tp", "ctx"),
        P("dp", "tp", "ctx"),
        P(("tp", "ctx"), None),
        P("tp", None),
    )
    return jax.shard_map(
        on_device,
        mesh=mesh,
        in_specs=placed,
        out_specs=(P("dp", "tp", "ctx"), P("dp", "tp", "ctx"), P(("tp", "ctx", "dp"), None)),
        check_vma=False,
    )
```

profile of v0, /device:TPU:1, one launch (start us, length us, event | category | flops | bytes accessed | tf_op | source)
XLA Modules:
  0.0 158.1 jit_solution(15856184088370610433)
XLA Ops:
  0.6 21.4 %all-to-all-start.1 = ((bf16[32,16,128]{2,1,0:T(8,128)(2,1)}), bf16[32,16,128]{2,1,0:T(8,128)(2,1)S(1)}, u32[]{:S(2)}, u32[]{:S(2)}) async-start(bf16[32,16,128]{2,1,0:T(8,128)(2,1)} %bitcast.156), calls=%async_computation.1 | async-start | bytes 262144 | tf_op jit(solution)/shard_map/all_to_all | solution.py:104
  22.4 1.0 multiply_bitcast_fusion
  24.8 0.8 fusion.49
  26.5 8.7 %all-to-all-done.1 = bf16[32,16,128]{2,1,0:T(8,128)(2,1)S(1)} async-done(((bf16[32,16,128]{2,1,0:T(8,128)(2,1)}), bf16[32,16,128]{2,1,0:T(8,128)(2,1)S(1)}, u32[]{:S(2)}, u32[]{:S(2)}) %all-to-all-start.1) | async-done | bytes 131104 | tf_op jit(solution)/shard_map/all_to_all | solution.py:104
  35.2 1.1 broadcast_in_dim.6
  36.3 6.5 %all-to-all-start = ((bf16[8,16,4096]{2,1,0:T(8,128)(2,1)}), bf16[8,16,4096]{2,1,0:T(8,128)(2,1)S(1)}, u32[]{:S(2)}, u32[]{:S(2)}) async-start(bf16[8,16,4096]{2,1,0:T(8,128)(2,1)} %broadcast_in_dim.6), calls=%async_computation | async-start | bytes 2097152 | tf_op jit(solution)/shard_map/all_to_all | solution.py:11
  43.6 0.8 convolution_subtract_fusion.5
  45.4 0.8 fusion.10
  46.3 1.6 %fusion.12 = f32[16,64,128]{2,1,0:T(8,128)} fusion(f32[64,16,128]{2,0,1:T(8,128)S(1)} %fusion.55, f32[64,16,128]{2,0,1:T(8,128)S(1)} %fusion.57, f32[64,128]{1,0:T(8,128)S(1)} %get-tuple-element.15, f32[64,128]{1,0:T(8,128)S(1)} %get-tuple-element.16), kind=kOutput, calls=%fused_computation.31 | convolution fusion | flops 201949184 | bytes 1638400 | tf_op jit(solution)/shard_map/cka,aj->ckj/dot_general | solution.py:48
  47.9 1.6 %convolution_add_fusion.4 = f32[16,64,128]{2,1,0:T(8,128)} fusion(f32[16,64,128]{2,1,0:T(8,128)S(1)} %fusion.10, f32[64,16,128]{2,0,1:T(8,128)S(1)} %fusion.55, f32[64,16,128]{2,0,1:T(8,128)S(1)} %fusion.57, f32[64,128]{1,0:T(8,128)S(1)} %get-tuple-element.15, f32[64,128]{1,0:T(8,128)S(1)} %get-tuple-element.16), kind=kOutput, calls=%fused_computation.12 | convolution fusion | flops 202080256 | bytes 2162688 | tf_op jit(solution)/shard_map/cka,aj->ckj/dot_general | solution.py:48
  49.6 22.5 %all-to-all-done = bf16[8,16,4096]{2,1,0:T(8,128)(2,1)S(1)} async-done(((bf16[8,16,4096]{2,1,0:T(8,128)(2,1)}), bf16[8,16,4096]{2,1,0:T(8,128)(2,1)S(1)}, u32[]{:S(2)}, u32[]{:S(2)}) %all-to-all-start) | async-done | bytes 1048608 | tf_op jit(solution)/shard_map/all_to_all | solution.py:11
  72.0 4.2 %fusion.35 = (bf16[512,128]{1,0:T(8,128)(2,1)}, f32[512,128]{1,0:T(8,128)}) fusion(bf16[1,512,128]{2,1,0:T(8,128)(2,1)S(1)} %copy-done.3, bf16[512,4096]{1,0:T(8,128)(2,1)} %param.9, bf16[128,4096]{1,0:T(8,128)(2,1)S(1)} %bitcast.151), kind=kOutput, calls=%fused_computation.67 | convolution fusion | flops 537067520 | bytes 5767168 | tf_op jit(solution)/shard_map/dot_general | solution.py:95
  76.2 4.2 %all-to-all-start.3 = ((bf16[32,16,128]{2,1,0:T(8,128)(2,1)}), bf16[32,16,128]{2,1,0:T(8,128)(2,1)S(1)}, u32[]{:S(2)}, u32[]{:S(2)}) async-start(bf16[32,16,128]{2,1,0:T(8,128)(2,1)} %bitcast.20), calls=%async_computation.3 | async-start | bytes 262144 | tf_op jit(solution)/shard_map/all_to_all | solution.py:103
  80.4 1.9 %convolution_subtract_fusion.4 = f32[16,64,128]{2,1,0:T(8,128)S(1)} fusion(f32[16,64,128]{2,1,0:T(8,128)} %fusion.12, f32[64,16,128]{2,0,1:T(8,128)S(1)} %fusion.55, f32[64,16,128]{2,0,1:T(8,128)S(1)} %fusion.57, f32[64,128]{1,0:T(8,128)S(1)} %get-tuple-element.15, f32[64,128]{1,0:T(8,128)S(1)} %get-tuple-element.16), kind=kOutput, calls=%fused_computation.14 | convolution fusion | flops 202096640 | bytes 2162688 | tf_op jit(solution)/shard_map/cka,aj->ckj/dot_general | solution.py:48
  82.3 11.2 %all-to-all-done.3 = bf16[32,16,128]{2,1,0:T(8,128)(2,1)S(1)} async-done(((bf16[32,16,128]{2,1,0:T(8,128)(2,1)}), bf16[32,16,128]{2,1,0:T(8,128)(2,1)S(1)}, u32[]{:S(2)}, u32[]{:S(2)}) %all-to-all-start.3) | async-done | bytes 131104 | tf_op jit(solution)/shard_map/all_to_all | solution.py:103
  94.6 0.8 fusion.51
  95.4 0.8 fusion.52
  96.2 0.8 convolution_add_fusion.2
  97.1 1.1 multiply_subtract_fusion
  98.2 0.8 fusion.66
  99.8 0.8 fusion.72
  103.9 0.8 convolution_subtract_fusion
  104.8 1.0 convolution_add_fusion.3
  105.8 0.8 convolution_subtract_fusion.3
  108.5 3.6 %all-to-all-start.2 = ((bf16[16,32,128]{2,0,1:T(8,128)(2,1)}), bf16[16,32,128]{2,0,1:T(8,128)(2,1)S(1)}, u32[]{:S(2)}, u32[]{:S(2)}) async-start(bf16[16,32,128]{2,0,1:T(8,128)(2,1)} %copy.15), calls=%async_computation.2 | async-start | bytes 262144 | tf_op jit(solution)/shard_map/all_to_all | solution.py:120
  112.1 0.8 convolution_add_fusion.1
  112.9 0.8 convolution_subtract_fusion.1
  116.1 9.3 %all-to-all-done.2 = bf16[16,32,128]{2,0,1:T(8,128)(2,1)S(1)} async-done(((bf16[16,32,128]{2,0,1:T(8,128)(2,1)}), bf16[16,32,128]{2,0,1:T(8,128)(2,1)S(1)}, u32[]{:S(2)}, u32[]{:S(2)}) %all-to-all-start.2) | async-done | bytes 131104 | tf_op jit(solution)/shard_map/all_to_all | solution.py:120
  125.4 3.6 %all-to-all-start.4 = ((bf16[16,32,128]{2,0,1:T(8,128)(2,1)}), bf16[16,32,128]{2,0,1:T(8,128)(2,1)S(1)}, u32[]{:S(2)}, u32[]{:S(2)}) async-start(bf16[16,32,128]{2,0,1:T(8,128)(2,1)} %copy.17), calls=%async_computation.4 | async-start | bytes 262144 | tf_op jit(solution)/shard_map/all_to_all | solution.py:121
  130.4 11.9 %all-to-all-done.4 = bf16[16,32,128]{2,0,1:T(8,128)(2,1)S(1)} async-done(((bf16[16,32,128]{2,0,1:T(8,128)(2,1)}), bf16[16,32,128]{2,0,1:T(8,128)(2,1)S(1)}, u32[]{:S(2)}, u32[]{:S(2)}) %all-to-all-start.4) | async-done | bytes 131104 | tf_op jit(solution)/shard_map/all_to_all | solution.py:121
  142.3 7.0 %all-to-all-start.5 = ((f32[4,4,4096]{2,1,0:T(4,128)}), f32[4,4,4096]{2,1,0:T(4,128)S(1)}, u32[]{:S(2)}, u32[]{:S(2)}) async-start(f32[4,4,4096]{2,1,0:T(4,128)} %mul.1006), calls=%async_computation.5 | async-start | bytes 524288 | tf_op jit(solution)/shard_map/all_to_all | solution.py:33
  150.0 6.7 %all-to-all-done.5 = f32[4,4,4096]{2,1,0:T(4,128)S(1)} async-done(((f32[4,4,4096]{2,1,0:T(4,128)}), f32[4,4,4096]{2,1,0:T(4,128)S(1)}, u32[]{:S(2)}, u32[]{:S(2)}) %all-to-all-start.5) | async-done | bytes 262176 | tf_op jit(solution)/shard_map/all_to_all | solution.py:33
  (36 shorter events, 16.9 us)
Async XLA Ops:
  0.6 34.6 %copy-start.2 = (bf16[1,16,4096]{2,1,0:T(8,128)(2,1)S(1)}, bf16[1,16,4096]{2,1,0:T(8,128)(2,1)}, u32[]{:S(2)}) copy-start(bf16[1,16,4096]{2,1,0:T(8,128)(2,1)} %param.5) | copy-start | bytes 393220
  0.6 34.6 %all-to-all-start.1 = ((bf16[32,16,128]{2,1,0:T(8,128)(2,1)}), bf16[32,16,128]{2,1,0:T(8,128)(2,1)S(1)}, u32[]{:S(2)}, u32[]{:S(2)}) async-start(bf16[32,16,128]{2,1,0:T(8,128)(2,1)} %bitcast.156), calls=%async_computation.1 | async-start | bytes 262144 | tf_op jit(solution)/shard_map/all_to_all | solution.py:104
  36.3 35.7 %all-to-all-start = ((bf16[8,16,4096]{2,1,0:T(8,128)(2,1)}), bf16[8,16,4096]{2,1,0:T(8,128)(2,1)S(1)}, u32[]{:S(2)}, u32[]{:S(2)}) async-start(bf16[8,16,4096]{2,1,0:T(8,128)(2,1)} %broadcast_in_dim.6), calls=%async_computation | async-start | bytes 2097152 | tf_op jit(solution)/shard_map/all_to_all | solution.py:11
  43.6 28.4 %copy-start.3 = (bf16[1,512,128]{2,1,0:T(8,128)(2,1)S(1)}, bf16[1,512,128]{2,1,0:T(8,128)(2,1)}, u32[]{:S(2)}) copy-start(bf16[1,512,128]{2,1,0:T(8,128)(2,1)} %param.6) | copy-start | bytes 393220
  76.2 17.4 %all-to-all-start.3 = ((bf16[32,16,128]{2,1,0:T(8,128)(2,1)}), bf16[32,16,128]{2,1,0:T(8,128)(2,1)S(1)}, u32[]{:S(2)}, u32[]{:S(2)}) async-start(bf16[32,16,128]{2,1,0:T(8,128)(2,1)} %bitcast.20), calls=%async_computation.3 | async-start | bytes 262144 | tf_op jit(solution)/shard_map/all_to_all | solution.py:103
  80.4 16.7 %copy-start = (f32[16,64,128]{2,1,0:T(8,128)S(1)}, f32[16,64,128]{2,1,0:T(8,128)}, u32[]{:S(2)}) copy-start(f32[16,64,128]{2,1,0:T(8,128)} %convolution_add_fusion.4) | copy-start | bytes 1572868
  108.5 16.9 %all-to-all-start.2 = ((bf16[16,32,128]{2,0,1:T(8,128)(2,1)}), bf16[16,32,128]{2,0,1:T(8,128)(2,1)S(1)}, u32[]{:S(2)}, u32[]{:S(2)}) async-start(bf16[16,32,128]{2,0,1:T(8,128)(2,1)} %copy.15), calls=%async_computation.2 | async-start | bytes 262144 | tf_op jit(solution)/shard_map/all_to_all | solution.py:120
  112.9 36.4 %copy-start.1 = (f32[512,128]{1,0:T(8,128)S(1)}, f32[512,128]{1,0:T(8,128)}, u32[]{:S(2)}) copy-start(f32[512,128]{1,0:T(8,128)} %get-tuple-element.14) | copy-start | bytes 786436
  125.4 16.9 %all-to-all-start.4 = ((bf16[16,32,128]{2,0,1:T(8,128)(2,1)}), bf16[16,32,128]{2,0,1:T(8,128)(2,1)S(1)}, u32[]{:S(2)}, u32[]{:S(2)}) async-start(bf16[16,32,128]{2,0,1:T(8,128)(2,1)} %copy.17), calls=%async_computation.4 | async-start | bytes 262144 | tf_op jit(solution)/shard_map/all_to_all | solution.py:121
  142.3 14.4 %all-to-all-start.5 = ((f32[4,4,4096]{2,1,0:T(4,128)}), f32[4,4,4096]{2,1,0:T(4,128)S(1)}, u32[]{:S(2)}, u32[]{:S(2)}) async-start(f32[4,4,4096]{2,1,0:T(4,128)} %mul.1006), calls=%async_computation.5 | async-start | bytes 524288 | tf_op jit(solution)/shard_map/all_to_all | solution.py:33
where the time goes:
time: 159 us; the launch traced here: 158 us
  waiting for transfers between devices  70.4 us (44%)
  starting transfers between devices  46.4 us (29%)
  matrix products  33.7 us (21%)
  local copies, waits for them, and re-layouts  4.01 us (3%)
  other arithmetic  2.63 us (2%)
    dot_general x36, matrix products, mix_einsum(): return jnp.einsum(form, left, right, precision=lax.Precision.HIGHEST)  29.5 us
    all_to_all x1, waiting for transfers between devices, from_everyone(): return lax.all_to_all(copies, axis, split_axis=0, concat_axis=0, tiled=True)  22.5 us
    all_to_all x1, starting transfers between devices, on_device(): lax.all_to_all(conv_local, 'ctx', split_axis=0, concat_axis=1, tiled=True)  21.4 us
    all_to_all x1, waiting for transfers between devices, on_device(): lax.all_to_all(conv_grad, 'ctx', split_axis=1, concat_axis=0, tiled=True)  11.9 us
    all_to_all x1, waiting for transfers between devices, on_device(): lax.all_to_all(gate_grad, 'ctx', split_axis=0, concat_axis=1, tiled=True)  11.2 us
    all_to_all x1, waiting for transfers between devices, on_device(): lax.all_to_all(conv_out, 'ctx', split_axis=1, concat_axis=0, tiled=True)  9.25 us
    all_to_all x1, waiting for transfers between devices, on_device(): lax.all_to_all(conv_local, 'ctx', split_axis=0, concat_axis=1, tiled=True)  8.74 us
    all_to_all x1, starting transfers between devices, sent_and_summed(): pieces = lax.all_to_all(split_up(array, dim, peers), axis, 0, 0, tiled=True)  6.97 us
  transfers between devices with their start and end apart: 6, of which 6 were waited for; matrix products, arithmetic and copies ran while one was open for 12% of the time, Pallas kernels for 0%

commit v1 on v0

v1 whole, which is shorter than its diff:
```python
import functools
import math

import jax
import jax.numpy as jnp
import numpy as np
from jax import lax
from jax.experimental import pallas as pl
from jax.experimental.pallas import tpu as pltpu
from jax.sharding import PartitionSpec as P

MESH = pl.DeviceIdType.MESH
LANES = 128
CHANS = 16
CHUNKS = 4


def wave(order, index):
    angle = 2.0 * math.pi * (index % order) / order
    return (math.cos(angle), math.sin(angle))


def plus(left, right):
    if left is None:
        return right
    if right is None:
        return left
    return left + right


def minus(left, right):
    if right is None:
        return left
    if left is None:
        return -right
    return left - right


def padded_spectrum(blocks):
    m = len(blocks)
    if m == 1:
        return [(blocks[0], None), (blocks[0], None)]
    even = padded_spectrum(blocks[0::2])
    odd = padded_spectrum(blocks[1::2])
    rows = [None] * (m + 1)
    rows[0] = (even[0][0] + odd[0][0], None)
    rows[m] = (even[0][0] - odd[0][0], None)
    for k in range(1, m // 2):
        cos, sin = wave(2 * m, k)
        odd_re, odd_im = odd[k]
        turn_re = odd_re * cos + odd_im * sin
        turn_im = odd_im * cos - odd_re * sin
        rows[k] = (even[k][0] + turn_re, even[k][1] + turn_im)
        rows[m - k] = (even[k][0] - turn_re, turn_im - even[k][1])
    rows[m // 2] = (even[m // 2][0], -odd[m // 2][0])
    return rows


def half_signal(rows):
    m = len(rows) - 1
    if m == 1:
        return [rows[0][0] + rows[1][0]]
    even, odd = [None] * (m // 2 + 1), [None] * (m // 2 + 1)
    even[0] = (rows[0][0] + rows[m][0], None)
    odd[0] = (rows[0][0] - rows[m][0], None)
    for k in range(1, m // 2):
        cos, sin = wave(2 * m, k)
        (low_re, low_im), (top_re, top_im) = rows[k], rows[m - k]
        even[k] = (low_re + top_re, low_im - top_im)
        diff_re, diff_im = low_re - top_re, low_im + top_im
        odd[k] = (diff_re * cos - diff_im * sin, diff_im * cos + diff_re * sin)
    even[m // 2] = (2.0 * rows[m // 2][0], None)
    odd[m // 2] = (-2.0 * rows[m // 2][1], None)
    blocks = [None] * m
    blocks[0::2] = half_signal(even)
    blocks[1::2] = half_signal(odd)
    return blocks


def in_two(table):
    high = table.astype(jnp.bfloat16)
    low = (table - np.asarray(high).astype(np.float64)).astype(jnp.bfloat16)
    return np.stack([np.asarray(high), np.asarray(low)])


def tables(blocks, scale):
    total = 2 * blocks * LANES
    rows = np.arange(blocks + 1)[:, None]
    lanes = np.arange(LANES)[None, :]
    angle = 2.0 * np.pi * (rows * lanes % total) / total
    twist = np.stack([np.cos(angle), -np.sin(angle)]).astype(np.float32)
    untwist = (np.stack([np.cos(angle), np.sin(angle)]) * scale).astype(np.float32)
    turn = 2.0 * np.pi * (lanes.T * lanes % LANES) / LANES
    cos, sin = np.cos(turn), np.sin(turn)
    ahead = in_two(np.block([[cos, -sin], [sin, cos]]))
    back = in_two(np.block([[cos, sin], [-sin, cos]]))
    return twist, untwist, ahead, back


def split_store(high, low, row, part, value):
    top = value.astype(jnp.bfloat16)
    rows = pl.ds(row * CHANS, CHANS)
    cols = pl.ds(part * LANES, LANES)
    high[rows, cols] = top
    low[rows, cols] = (value - top.astype(jnp.float32)).astype(jnp.bfloat16)


def inner(high, low, matrix, out):
    dot = functools.partial(jnp.dot, preferred_element_type=jnp.float32)
    out[...] = (
        dot(high[...], matrix[0]) + dot(low[...], matrix[0]) + dot(high[...], matrix[1])
    )


def cell(spectrum, row):
    rows = pl.ds(row * CHANS, CHANS)
    return spectrum[rows, pl.ds(0, LANES)], spectrum[rows, pl.ds(LANES, LANES)]


def ahead_transform(blocks, twist, matrix, high, low, out):
    for k, (re, im) in enumerate(padded_spectrum(blocks)):
        cos, sin = twist[0, pl.ds(k, 1), :], twist[1, pl.ds(k, 1), :]
        if im is None:
            split_store(high, low, k, 0, re * cos)
            split_store(high, low, k, 1, re * sin)
        else:
            split_store(high, low, k, 0, re * cos - im * sin)
            split_store(high, low, k, 1, re * sin + im * cos)
    inner(high, low, matrix, out)


def back_transform(product, count, untwist, matrix, high, low, out):
    for k in range(count + 1):
        re, im = product(k)
        split_store(high, low, k, 0, re)
        split_store(high, low, k, 1, im)
    inner(high, low, matrix, out)
    rows = []
    for k in range(count + 1):
        cos, sin = untwist[0, pl.ds(k, 1), :], untwist[1, pl.ds(k, 1), :]
        re, im = cell(out, k)
        real = re * cos - im * sin
        rows.append((real, None if k in (0, count) else re * sin + im * cos))
    return half_signal(rows)


def times(left, right):
    return (left[0] * right[0] - left[1] * right[1], left[0] * right[1] + left[1] * right[0])


def times_conj(left, right):
    return (left[0] * right[0] + left[1] * right[1], left[1] * right[0] - left[0] * right[1])


def kernel(
    n_ctx, n_tp, n_dp,
    grad_hbm, gate_hbm, conv_hbm, filt_hbm, weight_hbm,
    twist_hbm, untwist_hbm, ahead_hbm, back_hbm,
    gate_out, conv_grad_out, filt_grad_out,
    ring, gate_buf, conv_buf, filt_buf, weight, twist, untwist, ahead, back,
    unit, gate_send, out_send, grad_send, conv_in, gate_in, out_in, grad_in,
    high, low, spec_filt, spec_conv, spec_gate, spec_tmp, part_send, part_in,
    load_sem, ring_send, ring_recv, swap_send, swap_recv, part_send_sem, part_recv_sem,
):
    ctx, tp, dp = lax.axis_index("ctx"), lax.axis_index("tp"), lax.axis_index("dp")
    right, left = lax.rem(tp + 1, n_tp), lax.rem(tp + n_tp - 1, n_tp)

    barrier = pltpu.get_barrier_semaphore()
    for peer in (right, left):
        pl.semaphore_signal(barrier, inc=1, device_id={"tp": peer}, device_id_type=MESH)

    def greet(i, carry):
        peer = lax.rem(ctx + i, n_ctx)
        pl.semaphore_signal(barrier, inc=1, device_id={"ctx": peer}, device_id_type=MESH)
        return carry

    lax.fori_loop(1, n_ctx, greet, 0)
    for i in range(1, n_dp):
        peer = lax.rem(dp + i, n_dp)
        pl.semaphore_signal(barrier, inc=1, device_id={"dp": peer}, device_id_type=MESH)

    loads = [
        pltpu.make_async_copy(src, dst, load_sem.at[i])
        for i, (src, dst) in enumerate(
            [
                (grad_hbm, ring.at[tp]), (conv_hbm, conv_buf), (filt_hbm, filt_buf),
                (twist_hbm, twist), (ahead_hbm, ahead), (untwist_hbm, untwist),
                (back_hbm, back), (weight_hbm, weight), (gate_hbm, gate_buf),
            ]
        )
    ]
    for load in loads:
        load.start()
    loads[2].wait()
    loads[3].wait()
    loads[4].wait()
    ahead_transform(
        [filt_buf[:, pl.ds(j * LANES, LANES)] for j in range(n_ctx)],
        twist, ahead, high, low, spec_filt,
    )
    loads[0].wait()
    loads[1].wait()
    pl.semaphore_wait(barrier, 2 + n_ctx - 1 + n_dp - 1)

    width = ring.shape[2] // CHUNKS
    last = n_tp // 2 - 1

    def hop(way, step, chunk):
        origin = lax.rem(tp + step, n_tp) if way else lax.rem(tp + n_tp - step, n_tp)
        block = ring.at[origin, :, pl.ds(chunk * width, width)]
        return pltpu.make_async_remote_copy(
            src_ref=block,
            dst_ref=block,
            send_sem=ring_send.at[way, step, chunk],
            recv_sem=ring_recv.at[way, step, chunk],
            device_id={"tp": left if way else right},
            device_id_type=MESH,
        )

    def arrival(way, step, chunk):
        origin = lax.rem(tp + step + 1, n_tp) if way else lax.rem(tp + n_tp - step - 1, n_tp)
        block = ring.at[origin, :, pl.ds(chunk * width, width)]
        return pltpu.make_async_remote_copy(
            src_ref=block,
            dst_ref=block,
            send_sem=ring_send.at[way, step, chunk],
            recv_sem=ring_recv.at[way, step, chunk],
            device_id={"tp": left if way else right},
            device_id_type=MESH,
        )

    def ways(step, chunk):
        if step < last:
            return (0, 1)
        return (0,) if chunk < CHUNKS // 2 else (1,)

    sends = []

    def forward(way, step, chunk):
        copy = hop(way, step, chunk)
        copy.start()
        sends.append(copy)

    for chunk in range(CHUNKS):
        for way in ways(0, chunk):
            forward(way, 0, chunk)

    mine = pl.ds(pl.multiple_of(ctx * CHANS, CHANS), CHANS)

    def exchange(which, source, target):
        def send(i, carry):
            peer = lax.rem(ctx + i, n_ctx)
            theirs = pl.ds(pl.multiple_of(peer * CHANS, CHANS), CHANS)
            pltpu.make_async_remote_copy(
                src_ref=source.at[theirs, :],
                dst_ref=target.at[mine, :],
                send_sem=swap_send.at[which],
                recv_sem=swap_recv.at[which],
                device_id={"ctx": peer},
                device_id_type=MESH,
            ).start()
            return carry

        lax.fori_loop(1, n_ctx, send, 0)
        target[mine, :] = source[mine, :]

    def exchanged(which, source, target):
        rows = pl.ds(0, (n_ctx - 1) * CHANS)
        return pltpu.make_async_remote_copy(
            src_ref=source.at[rows, :],
            dst_ref=target.at[rows, :],
            send_sem=swap_send.at[which],
            recv_sem=swap_recv.at[which],
            device_id={"ctx": lax.rem(ctx + 1, n_ctx)},
            device_id_type=MESH,
        )

    def token_blocks(buf):
        return [
            buf[pl.ds(j * CHANS, CHANS), :].astype(jnp.float32) for j in range(n_ctx)
        ]

    def put_blocks(buf, blocks):
        for j, block in enumerate(blocks):
            buf[pl.ds(j * CHANS, CHANS), :] = block.astype(jnp.bfloat16)

    exchange(0, conv_buf, conv_in)

    for step in range(last):
        for chunk in range(CHUNKS):
            for way in (0, 1):
                arrival(way, step, chunk).wait_recv()
                if way in ways(step + 1, chunk):
                    forward(way, step + 1, chunk)
    for chunk in range(CHUNKS):
        for way in ways(last, chunk):
            arrival(way, last, chunk).wait_recv()

    loads[7].wait()
    loads[8].wait()
    tokens = ring[...].reshape(LANES, ring.shape[2])
    tile = min(128, unit.shape[0])

    def project(i, carry):
        rows = pl.ds(pl.multiple_of(i * tile, tile), tile)
        grad = lax.dot_general(
            weight[rows, :], tokens, (((1,), (1,)), ((), ())),
            preferred_element_type=jnp.float32,
        )
        unit[rows, :] = grad
        gate_send[rows, :] = (grad * gate_buf[rows, :].astype(jnp.float32)).astype(jnp.bfloat16)
        return carry

    lax.fori_loop(0, unit.shape[0] // tile, project, 0)
    exchange(1, gate_send, gate_in)

    exchanged(0, conv_buf, conv_in).wait_recv()
    ahead_transform(token_blocks(conv_in), twist, ahead, high, low, spec_conv)
    loads[5].wait()
    loads[6].wait()
    put_blocks(out_send, back_transform(
        lambda k: times(cell(spec_filt, k), cell(spec_conv, k)),
        n_ctx, untwist, back, high, low, spec_tmp,
    ))
    exchange(2, out_send, out_in)

    exchanged(1, gate_send, gate_in).wait_recv()
    ahead_transform(token_blocks(gate_in), twist, ahead, high, low, spec_gate)
    put_blocks(grad_send, back_transform(
        lambda k: times_conj(cell(spec_gate, k), cell(spec_filt, k)),
        n_ctx, untwist, back, high, low, spec_tmp,
    ))
    exchange(3, grad_send, grad_in)

    per = CHANS // n_dp
    group = 8 // per
    filt_grads = back_transform(
        lambda k: times_conj(cell(spec_gate, k), cell(spec_conv, k)),
        n_ctx, untwist, back, high, low, spec_tmp,
    )
    for piece in range(n_dp):
        for j, block in enumerate(filt_grads):
            part_send[piece, j // group, pl.ds(j % group * per, per), :] = block[
                piece * per : (piece + 1) * per, :
            ]

    def part(i):
        peer = lax.rem(dp + i, n_dp)
        return pltpu.make_async_remote_copy(
            src_ref=part_send.at[peer],
            dst_ref=part_in.at[i - 1],
            send_sem=part_send_sem.at[i - 1],
            recv_sem=part_recv_sem.at[i - 1],
            device_id={"dp": peer},
            device_id_type=MESH,
        )

    parts = [part(i) for i in range(1, n_dp)]
    for copy in parts:
        copy.start()

    exchanged(2, out_send, out_in).wait_recv()
    gate_out[...] = (unit[...] * out_in[...].astype(jnp.float32)).astype(jnp.bfloat16)

    for copy in parts:
        copy.wait_recv()
    total = part_send[dp]
    for i in range(n_dp - 1):
        total = total + part_in[i]
    for j in range(n_ctx):
        filt_grad_out[:, pl.ds(j * LANES, LANES)] = total[
            j // group, j % group * per : (j % group + 1) * per, :
        ]

    exchanged(3, grad_send, grad_in).wait_recv()
    conv_grad_out[...] = grad_in[...]

    for copy in sends:
        copy.wait_send()
    for which, source, target in (
        (0, conv_buf, conv_in), (1, gate_send, gate_in),
        (2, out_send, out_in), (3, grad_send, grad_in),
    ):
        exchanged(which, source, target).wait_send()
    for copy in parts:
        copy.wait_send()


def on_device(sizes, out_grad, gate_in, conv_in, filter_raw, out_weight):
    n_ctx, n_tp, n_dp = sizes
    bf16, f32 = jnp.bfloat16, jnp.float32
    length = filter_raw.shape[1]
    depth = out_weight.shape[1]
    local = gate_in.shape[1]
    scale = 1.0 / math.sqrt(length) / (2 * length)
    twist, untwist, ahead, back = tables(n_ctx, scale)
    rows = (n_ctx + 1) * CHANS
    per = CHANS // n_dp
    group = 8 // per
    vmem = pltpu.VMEM
    dma = pltpu.SemaphoreType.DMA
    whole = pl.BlockSpec(memory_space=pltpu.VMEM)
    grad, gate, filt = pl.pallas_call(
        functools.partial(kernel, n_ctx, n_tp, n_dp),
        out_shape=(
            jax.ShapeDtypeStruct((local, LANES), bf16),
            jax.ShapeDtypeStruct((local, LANES), bf16),
            jax.ShapeDtypeStruct((per, length), f32),
        ),
        in_specs=[pl.BlockSpec(memory_space=pl.ANY)] * 9,
        out_specs=(whole, whole, whole),
        scratch_shapes=[
            vmem((n_tp, 16, depth), bf16),
            vmem((local, LANES), bf16),
            vmem((local, LANES), bf16),
            vmem((CHANS, length), f32),
            vmem((local, depth), bf16),
            vmem(twist.shape, f32),
            vmem(untwist.shape, f32),
            vmem(ahead.shape, bf16),
            vmem(back.shape, bf16),
            vmem((local, LANES), f32),
            *[vmem((local, LANES), bf16)] * 7,
            vmem((rows, 2 * LANES), bf16),
            vmem((rows, 2 * LANES), bf16),
            *[vmem((rows, 2 * LANES), f32)] * 4,
            vmem((n_dp, n_ctx // group, 8, LANES), f32),
            vmem((n_dp - 1, n_ctx // group, 8, LANES), f32),
            dma((9,)),
            dma((2, n_tp // 2, CHUNKS)),
            dma((2, n_tp // 2, CHUNKS)),
            dma((4,)),
            dma((4,)),
            dma((n_dp - 1,)),
            dma((n_dp - 1,)),
        ],
        compiler_params=pltpu.CompilerParams(collective_id=0, has_side_effects=True),
    )(
        out_grad[0], gate_in[0], conv_in[0], filter_raw, out_weight,
        jnp.asarray(twist), jnp.asarray(untwist), jnp.asarray(ahead), jnp.asarray(back),
    )
    return grad[None], gate[None], filt


def solution(mesh):
    sizes = (mesh.shape["ctx"], mesh.shape["tp"], mesh.shape["dp"])
    placed = (
        P("dp", ("ctx", "tp"), None),
        P("dp", "tp", "ctx"),
        P("dp", "tp", "ctx"),
        P(("tp", "ctx"), None),
        P("tp", None),
    )
    return jax.shard_map(
        functools.partial(on_device, sizes),
        mesh=mesh,
        in_specs=placed,
        out_specs=(P("dp", "tp", "ctx"), P("dp", "tp", "ctx"), P(("tp", "ctx", "dp"), None)),
        check_vma=False,
    )
```

time: 159 us -> 65.6 us (0.41)
  waiting for transfers between devices: 70.4 us -> 0 us
  Pallas kernels: 0 us -> 59.8 us
  starting transfers between devices: 46.4 us -> 0 us
  matrix products: 33.7 us -> 0 us
  other arithmetic: 2.63 us -> 0 us
    all_to_all x6 -> x0, waiting for transfers between devices: 70.4 us -> none  [the longest x1 22.5 us: from_everyone(): return lax.all_to_all(copies, axis, split_axis=0, concat_axis=0, tiled=True)]
    pallas_call x0 -> x1, Pallas kernels: none -> 59.8 us  [on_device(): pl.pallas_call(functools.partial(kernel, n_ctx, n_tp, n_dp), out_shape=(j...]
    all_to_all x6 -> x0, starting transfers between devices: 46.4 us -> none  [the longest x1 21.4 us: on_device(): lax.all_to_all(conv_local, 'ctx', split_axis=0, concat_axis=1, tiled=True)]
    dot_general x37 -> x0, matrix products: 33.7 us -> none  [the longest x36 29.5 us: mix_einsum(): return jnp.einsum(form, left, right, precision=lax.Precision.HIGHEST)]
    unnamed x10 -> x3, local copies, waits for them, and re-layouts: 0.73 us -> 4.61 us
  transfers between devices with their start and end apart: 6 -> 0, of which waited for: 6 -> 0; matrix products, arithmetic and copies ran while one was open for 12% -> 0% of each run, Pallas kernels for 0% -> 0%
where the time goes in v1:
time: 65.6 us; the launch traced here: 65.1 us
  Pallas kernels  59.8 us (91%)
  local copies, waits for them, and re-layouts  4.61 us (7%)
    pallas_call x1, Pallas kernels, on_device(): pl.pallas_call(functools.partial(kernel, n_ctx, n_tp, n_dp), out_shape=(j...  59.8 us
    unnamed x3, local copies, waits for them, and re-layouts  4.61 us

profile of v1, /device:TPU:1, one launch (start us, length us, event | category | flops | bytes accessed | tf_op | source)
XLA Modules:
  0.0 65.1 jit_solution(15043481895912094001)
XLA Ops:
  0.6 59.8 %shard_map.112 = (bf16[512,128]{1,0:T(8,128)(2,1)}, bf16[512,128]{1,0:T(8,128)(2,1)}, f32[4,4096]{1,0:T(4,128)}) custom-call(bf16[16,4096]{1,0:T(8,128)(2,1)} %bitcast.5, bf16[512,128]{1,0:T(8,128)(2,1)} %bitcast.6, bf16[512,128]{1,0:T(8,128)(2,1)} %bitcast.7, f32[16,4096]{1,0:T(8,128)} %filt_hbm.1, bf16[512,4096]{1,0:T(8,128)(2,1)} %weight_hbm.1, ...), custom_call_target="tpu_custom_call" | custom-call | tf_op jit(solution)/shard_map/pallas_call | solution.py:403
  60.4 1.6 %copy.15 = bf16[1,512,128]{2,1,0:T(8,128)(2,1)} copy(bf16[1,512,128]{2,1,0:T(8,128)(2,1)} %bitcast.9) | data formatting | bytes 262144
  62.0 1.6 %copy.16 = bf16[1,512,128]{2,1,0:T(8,128)(2,1)} copy(bf16[1,512,128]{2,1,0:T(8,128)(2,1)} %bitcast.8) | data formatting | bytes 262144
  63.6 1.5 %copy.17 = f32[4,4096]{1,0:T(4,128)} copy(f32[4,4096]{1,0:T(4,128)} %get-tuple-element.14) | data formatting | bytes 131072

commit v2 on v1

--- a/solution.py
+++ b/solution.py
@@ -13,6 +13,8 @@
 LANES = 128
 CHANS = 16
 CHUNKS = 4
+FINISH_VMEM = 1024 * 1024
+MAIN_VMEM = 65536000
 
 
 def wave(order, index):
@@ -161,23 +163,36 @@
     unit, gate_send, out_send, grad_send, conv_in, gate_in, out_in, grad_in,
     high, low, spec_filt, spec_conv, spec_gate, spec_tmp, part_send, part_in,
     load_sem, ring_send, ring_recv, swap_send, swap_recv, part_send_sem, part_recv_sem,
+    news,
 ):
     ctx, tp, dp = lax.axis_index("ctx"), lax.axis_index("tp"), lax.axis_index("dp")
     right, left = lax.rem(tp + 1, n_tp), lax.rem(tp + n_tp - 1, n_tp)
 
+    n_y, n_z = n_ctx // 4, 2 * n_dp
+    y, z, core = ctx // 4, lax.rem(ctx // 2, 2) * n_dp + dp, lax.rem(ctx, 2)
+
+    def place(y_at, z_at, core_at):
+        return {"ctx": y_at * 4 + z_at // n_dp * 2 + core_at, "dp": lax.rem(z_at, n_dp)}
+
+    y_sides = [place(lax.rem(y + d, n_y), z, core) for d in (1, n_y - 1)]
+    z_sides = [place(y, lax.rem(z + d, n_z), core) for d in (1, n_z - 1)]
+    other_core = [place(y, z, 1 - core)]
+    tp_sides = [{"tp": right}, {"tp": left}]
+
     barrier = pltpu.get_barrier_semaphore()
-    for peer in (right, left):
-        pl.semaphore_signal(barrier, inc=1, device_id={"tp": peer}, device_id_type=MESH)
-
-    def greet(i, carry):
-        peer = lax.rem(ctx + i, n_ctx)
-        pl.semaphore_signal(barrier, inc=1, device_id={"ctx": peer}, device_id_type=MESH)
-        return carry
-
-    lax.fori_loop(1, n_ctx, greet, 0)
-    for i in range(1, n_dp):
-        peer = lax.rem(dp + i, n_dp)
-        pl.semaphore_signal(barrier, inc=1, device_id={"dp": peer}, device_id_type=MESH)
+    close_by = tp_sides + y_sides + z_sides + other_core
+    for peer in close_by:
+        pl.semaphore_signal(barrier, inc=1, device_id=peer, device_id_type=MESH)
+    rounds = [y_sides] * (n_y // 2 - 1) + [z_sides] * (n_z // 2) + [other_core]
+
+    def tell(at):
+        for peer in rounds[at]:
+            pl.semaphore_signal(news.at[at], inc=1, device_id=peer, device_id_type=MESH)
+
+    def hear(at):
+        pl.semaphore_wait(news.at[at], len(rounds[at]))
+        if at + 1 < len(rounds):
+            tell(at + 1)
 
     loads = [
         pltpu.make_async_copy(src, dst, load_sem.at[i])
@@ -191,25 +206,17 @@
     ]
     for load in loads:
         load.start()
-    loads[2].wait()
-    loads[3].wait()
-    loads[4].wait()
-    ahead_transform(
-        [filt_buf[:, pl.ds(j * LANES, LANES)] for j in range(n_ctx)],
-        twist, ahead, high, low, spec_filt,
-    )
-    loads[0].wait()
-    loads[1].wait()
-    pl.semaphore_wait(barrier, 2 + n_ctx - 1 + n_dp - 1)
+    pl.semaphore_wait(barrier, len(close_by))
 
     width = ring.shape[2] // CHUNKS
     last = n_tp // 2 - 1
 
     def hop(way, step, chunk):
         origin = lax.rem(tp + step, n_tp) if way else lax.rem(tp + n_tp - step, n_tp)
-        block = ring.at[origin, :, pl.ds(chunk * width, width)]
+        cols = pl.ds(chunk * width, width)
+        block = ring.at[origin, :, cols]
         return pltpu.make_async_remote_copy(
-            src_ref=block,
+            src_ref=block if step else grad_hbm.at[:, cols],
             dst_ref=block,
             send_sem=ring_send.at[way, step, chunk],
             recv_sem=ring_recv.at[way, step, chunk],
@@ -244,6 +251,17 @@
     for chunk in range(CHUNKS):
         for way in ways(0, chunk):
             forward(way, 0, chunk)
+    tell(0)
+
+    loads[2].wait()
+    loads[3].wait()
+    loads[4].wait()
+    ahead_transform(
+        [filt_buf[:, pl.ds(j * LANES, LANES)] for j in range(n_ctx)],
+        twist, ahead, high, low, spec_filt,
+    )
+    loads[0].wait()
+    loads[1].wait()
 
     mine = pl.ds(pl.multiple_of(ctx * CHANS, CHANS), CHANS)
 
@@ -284,14 +302,18 @@
         for j, block in enumerate(blocks):
             buf[pl.ds(j * CHANS, CHANS), :] = block.astype(jnp.bfloat16)
 
-    exchange(0, conv_buf, conv_in)
-
+    heard = 0
     for step in range(last):
         for chunk in range(CHUNKS):
             for way in (0, 1):
                 arrival(way, step, chunk).wait_recv()
                 if way in ways(step + 1, chunk):
                     forward(way, step + 1, chunk)
+            if heard < len(rounds):
+                hear(heard)
+                heard += 1
+                if heard == len(rounds):
+                    exchange(0, conv_buf, conv_in)
     for chunk in range(CHUNKS):
         for way in ways(last, chunk):
             arrival(way, last, chunk).wait_recv()
@@ -333,7 +355,7 @@
     exchange(3, grad_send, grad_in)
 
     per = CHANS // n_dp
-    group = 8 // per
+    group = max(8 // per, 1)
     filt_grads = back_transform(
         lambda k: times_conj(cell(spec_gate, k), cell(spec_conv, k)),
         n_ctx, untwist, back, high, low, spec_tmp,
@@ -386,6 +408,17 @@
         copy.wait_send()
 
 
+def hand_over(*refs):
+    half = len(refs) // 2
+    copies = [
+        pltpu.make_async_copy(refs[i], refs[half + i], refs[-1].at[i]) for i in range(half)
+    ]
+    for copy in copies:
+        copy.start()
+    for copy in copies:
+        copy.wait()
+
+
 def on_device(sizes, out_grad, gate_in, conv_in, filter_raw, out_weight):
     n_ctx, n_tp, n_dp = sizes
     bf16, f32 = jnp.bfloat16, jnp.float32
@@ -396,7 +429,7 @@
     twist, untwist, ahead, back = tables(n_ctx, scale)
     rows = (n_ctx + 1) * CHANS
     per = CHANS // n_dp
-    group = 8 // per
+    group = max(8 // per, 1)
     vmem = pltpu.VMEM
     dma = pltpu.SemaphoreType.DMA
     whole = pl.BlockSpec(memory_space=pltpu.VMEM)
@@ -407,7 +440,7 @@
             jax.ShapeDtypeStruct((local, LANES), bf16),
             jax.ShapeDtypeStruct((per, length), f32),
         ),
-        in_specs=[pl.BlockSpec(memory_space=pl.ANY)] * 9,
+        in_specs=[pl.BlockSpec(memory_space=pltpu.HBM)] * 9,
         out_specs=(whole, whole, whole),
         scratch_shapes=[
             vmem((n_tp, 16, depth), bf16),
@@ -433,12 +466,23 @@
             dma((4,)),
             dma((n_dp - 1,)),
             dma((n_dp - 1,)),
+            pltpu.SemaphoreType.REGULAR((n_ctx // 8 - 1 + n_dp + 1,)),
         ],
-        compiler_params=pltpu.CompilerParams(collective_id=0, has_side_effects=True),
+        compiler_params=pltpu.CompilerParams(
+            collective_id=0, has_side_effects=True, vmem_limit_bytes=MAIN_VMEM
+        ),
     )(
         out_grad[0], gate_in[0], conv_in[0], filter_raw, out_weight,
         jnp.asarray(twist), jnp.asarray(untwist), jnp.asarray(ahead), jnp.asarray(back),
     )
+    grad, gate, filt = pl.pallas_call(
+        hand_over,
+        out_shape=tuple(jax.ShapeDtypeStruct(a.shape, a.dtype) for a in (grad, gate, filt)),
+        in_specs=[pl.BlockSpec(memory_space=pl.ANY)] * 3,
+        out_specs=(pl.BlockSpec(memory_space=pltpu.HBM),) * 3,
+        scratch_shapes=[dma((3,))],
+        compiler_params=pltpu.CompilerParams(vmem_limit_bytes=FINISH_VMEM),
+    )(grad, gate, filt)
     return grad[None], gate[None], filt
 
 

time: 65.6 us -> 69.2 us (1.055)
  Pallas kernels: 59.8 us -> 65.7 us
  local copies, waits for them, and re-layouts: 4.61 us -> 2.64 us
    pallas_call x1, Pallas kernels: 59.8 us -> 64.9 us  [on_device(): pl.pallas_call(functools.partial(kernel, n_ctx, n_tp, n_dp), out_shape=(j...]
    unnamed x3 -> x6, local copies, waits for them, and re-layouts: 4.61 us -> 2.64 us
    pallas_call x0 -> x1, Pallas kernels: none -> 0.74 us  [on_device(): pl.pallas_call(hand_over, out_shape=tuple((jax.ShapeDtypeStruct(a.shape,...]
where the time goes in v2:
time: 69.2 us; the launch traced here: 68.9 us
  Pallas kernels  65.7 us (95%)
  local copies, waits for them, and re-layouts  2.64 us (4%)
    pallas_call x1, Pallas kernels, on_device(): pl.pallas_call(functools.partial(kernel, n_ctx, n_tp, n_dp), out_shape=(j...  64.9 us
    unnamed x6, local copies, waits for them, and re-layouts  2.64 us

profile of v2, /device:TPU:1, one launch (start us, length us, event | category | flops | bytes accessed | tf_op | source)
XLA Modules:
  0.0 68.9 jit_solution(6636149021811021781)
XLA Ops:
  0.6 64.9 %shard_map.112 = (bf16[512,128]{1,0:T(8,128)(2,1)}, bf16[512,128]{1,0:T(8,128)(2,1)}, f32[4,4096]{1,0:T(4,128)}) custom-call(bf16[16,4096]{1,0:T(8,128)(2,1)} %bitcast.5, bf16[512,128]{1,0:T(8,128)(2,1)} %bitcast.6, bf16[512,128]{1,0:T(8,128)(2,1)} %bitcast.7, f32[16,4096]{1,0:T(8,128)} %filt_hbm.1, bf16[512,4096]{1,0:T(8,128)(2,1)} %weight_hbm.1, ...), custom_call_target="tpu_custom_call" | custom-call | tf_op jit(solution)/shard_map/pallas_call | solution.py:436
  65.6 0.0 copy-start
  65.6 0.9 %copy-done = bf16[512,128]{1,0:T(8,128)(2,1)S(1)} copy-done((bf16[512,128]{1,0:T(8,128)(2,1)S(1)}, bf16[512,128]{1,0:T(8,128)(2,1)}, u32[]{:S(2)}) %copy-start) | copy-done | bytes 131096
  66.5 0.0 copy-start.1
  66.5 0.9 %copy-done.1 = bf16[512,128]{1,0:T(8,128)(2,1)S(1)} copy-done((bf16[512,128]{1,0:T(8,128)(2,1)S(1)}, bf16[512,128]{1,0:T(8,128)(2,1)}, u32[]{:S(2)}) %copy-start.1) | copy-done | bytes 131096
  67.4 0.0 copy-start.2
  67.4 0.8 %copy-done.2 = f32[4,4096]{1,0:T(4,128)S(1)} copy-done((f32[4,4096]{1,0:T(4,128)S(1)}, f32[4,4096]{1,0:T(4,128)}, u32[]{:S(2)}) %copy-start.2) | copy-done | bytes 65560
  68.2 0.7 %shard_map.113 = (bf16[512,128]{1,0:T(8,128)(2,1)}, bf16[512,128]{1,0:T(8,128)(2,1)}, f32[4,4096]{1,0:T(4,128)}) custom-call(bf16[512,128]{1,0:T(8,128)(2,1)S(1)} %copy-done, bf16[512,128]{1,0:T(8,128)(2,1)S(1)} %copy-done.1, f32[4,4096]{1,0:T(4,128)S(1)} %copy-done.2), custom_call_target="tpu_custom_call" | custom-call | tf_op jit(solution)/shard_map/pallas_call | solution.py:478
Async XLA Ops:
  65.6 0.9 %copy-start = (bf16[512,128]{1,0:T(8,128)(2,1)S(1)}, bf16[512,128]{1,0:T(8,128)(2,1)}, u32[]{:S(2)}) copy-start(bf16[512,128]{1,0:T(8,128)(2,1)} %get-tuple-element.9.refs_0_) | copy-start | bytes 393220
  66.5 0.9 %copy-start.1 = (bf16[512,128]{1,0:T(8,128)(2,1)S(1)}, bf16[512,128]{1,0:T(8,128)(2,1)}, u32[]{:S(2)}) copy-start(bf16[512,128]{1,0:T(8,128)(2,1)} %get-tuple-element.10.refs_1_) | copy-start | bytes 393220
  67.4 0.8 %copy-start.2 = (f32[4,4096]{1,0:T(4,128)S(1)}, f32[4,4096]{1,0:T(4,128)}, u32[]{:S(2)}) copy-start(f32[4,4096]{1,0:T(4,128)} %get-tuple-element.11.refs_2_) | copy-start | bytes 196612

commit v3 on v2

--- a/solution.py
+++ b/solution.py
@@ -14,7 +14,7 @@
 CHANS = 16
 CHUNKS = 4
 FINISH_VMEM = 1024 * 1024
-MAIN_VMEM = 65536000
+MAIN_VMEM = 64000 * 1024
 
 
 def wave(order, index):
@@ -161,7 +161,7 @@
     gate_out, conv_grad_out, filt_grad_out,
     ring, gate_buf, conv_buf, filt_buf, weight, twist, untwist, ahead, back,
     unit, gate_send, out_send, grad_send, conv_in, gate_in, out_in, grad_in,
-    high, low, spec_filt, spec_conv, spec_gate, spec_tmp, part_send, part_in,
+    high, low, spec_filt, spec_conv, spec_gate, spec_tmp, part_own, part_send, part_in,
     load_sem, ring_send, ring_recv, swap_send, swap_recv, part_send_sem, part_recv_sem,
     news,
 ):
@@ -174,25 +174,16 @@
     def place(y_at, z_at, core_at):
         return {"ctx": y_at * 4 + z_at // n_dp * 2 + core_at, "dp": lax.rem(z_at, n_dp)}
 
-    y_sides = [place(lax.rem(y + d, n_y), z, core) for d in (1, n_y - 1)]
-    z_sides = [place(y, lax.rem(z + d, n_z), core) for d in (1, n_z - 1)]
-    other_core = [place(y, z, 1 - core)]
-    tp_sides = [{"tp": right}, {"tp": left}]
+    z_line = [place(y, lax.rem(z + d, n_z), core) for d in range(1, n_z)]
+    y_lines = [
+        place(lax.rem(y + d, n_y), z, lax.rem(core + c, 2))
+        for d in range(n_y) for c in (0, 1) if d or c
+    ]
 
     barrier = pltpu.get_barrier_semaphore()
-    close_by = tp_sides + y_sides + z_sides + other_core
-    for peer in close_by:
+    first = [{"tp": right}, {"tp": left}] + y_lines + z_line
+    for peer in first:
         pl.semaphore_signal(barrier, inc=1, device_id=peer, device_id_type=MESH)
-    rounds = [y_sides] * (n_y // 2 - 1) + [z_sides] * (n_z // 2) + [other_core]
-
-    def tell(at):
-        for peer in rounds[at]:
-            pl.semaphore_signal(news.at[at], inc=1, device_id=peer, device_id_type=MESH)
-
-    def hear(at):
-        pl.semaphore_wait(news.at[at], len(rounds[at]))
-        if at + 1 < len(rounds):
-            tell(at + 1)
 
     loads = [
         pltpu.make_async_copy(src, dst, load_sem.at[i])
@@ -206,7 +197,7 @@
     ]
     for load in loads:
         load.start()
-    pl.semaphore_wait(barrier, len(close_by))
+    pl.semaphore_wait(barrier, len(first))
 
     width = ring.shape[2] // CHUNKS
     last = n_tp // 2 - 1
@@ -241,6 +232,7 @@
             return (0, 1)
         return (0,) if chunk < CHUNKS // 2 else (1,)
 
+    orders = (range(CHUNKS), [(c + CHUNKS // 2) % CHUNKS for c in range(CHUNKS)])
     sends = []
 
     def forward(way, step, chunk):
@@ -248,10 +240,11 @@
         copy.start()
         sends.append(copy)
 
-    for chunk in range(CHUNKS):
-        for way in ways(0, chunk):
-            forward(way, 0, chunk)
-    tell(0)
+    for turn in range(CHUNKS):
+        for way in (0, 1):
+            forward(way, 0, orders[way][turn])
+    for peer in z_line:
+        pl.semaphore_signal(news, inc=1, device_id=peer, device_id_type=MESH)
 
     loads[2].wait()
     loads[3].wait()
@@ -302,21 +295,19 @@
         for j, block in enumerate(blocks):
             buf[pl.ds(j * CHANS, CHANS), :] = block.astype(jnp.bfloat16)
 
-    heard = 0
     for step in range(last):
-        for chunk in range(CHUNKS):
+        for turn in range(CHUNKS):
             for way in (0, 1):
+                chunk = orders[way][turn]
                 arrival(way, step, chunk).wait_recv()
                 if way in ways(step + 1, chunk):
                     forward(way, step + 1, chunk)
-            if heard < len(rounds):
-                hear(heard)
-                heard += 1
-                if heard == len(rounds):
-                    exchange(0, conv_buf, conv_in)
-    for chunk in range(CHUNKS):
-        for way in ways(last, chunk):
-            arrival(way, last, chunk).wait_recv()
+            if step == 0 and turn == 1:
+                pl.semaphore_wait(news, len(z_line))
+                exchange(0, conv_buf, conv_in)
+    for turn in range(CHUNKS // 2):
+        for way in (0, 1):
+            arrival(way, last, orders[way][turn]).wait_recv()
 
     loads[7].wait()
     loads[8].wait()
@@ -355,16 +346,17 @@
     exchange(3, grad_send, grad_in)
 
     per = CHANS // n_dp
-    group = max(8 // per, 1)
+    group = n_dp
     filt_grads = back_transform(
         lambda k: times_conj(cell(spec_gate, k), cell(spec_conv, k)),
         n_ctx, untwist, back, high, low, spec_tmp,
     )
     for piece in range(n_dp):
         for j, block in enumerate(filt_grads):
-            part_send[piece, j // group, pl.ds(j % group * per, per), :] = block[
+            part_own[piece, j // group, pl.ds(j % group * per, per), :] = block[
                 piece * per : (piece + 1) * per, :
             ]
+    part_send[...] = part_own[...].astype(jnp.bfloat16)
 
     def part(i):
         peer = lax.rem(dp + i, n_dp)
@@ -386,9 +378,9 @@
 
     for copy in parts:
         copy.wait_recv()
-    total = part_send[dp]
+    total = part_own[dp]
     for i in range(n_dp - 1):
-        total = total + part_in[i]
+        total = total + part_in[i].astype(jnp.float32)
     for j in range(n_ctx):
         filt_grad_out[:, pl.ds(j * LANES, LANES)] = total[
             j // group, j % group * per : (j % group + 1) * per, :
@@ -429,16 +421,15 @@
     twist, untwist, ahead, back = tables(n_ctx, scale)
     rows = (n_ctx + 1) * CHANS
     per = CHANS // n_dp
-    group = max(8 // per, 1)
     vmem = pltpu.VMEM
     dma = pltpu.SemaphoreType.DMA
     whole = pl.BlockSpec(memory_space=pltpu.VMEM)
     grad, gate, filt = pl.pallas_call(
         functools.partial(kernel, n_ctx, n_tp, n_dp),
         out_shape=(
-            jax.ShapeDtypeStruct((local, LANES), bf16),
-            jax.ShapeDtypeStruct((local, LANES), bf16),
-            jax.ShapeDtypeStruct((per, length), f32),
+            vmem((local, LANES), bf16),
+            vmem((local, LANES), bf16),
+            vmem((per, length), f32),
         ),
         in_specs=[pl.BlockSpec(memory_space=pltpu.HBM)] * 9,
         out_specs=(whole, whole, whole),
@@ -457,8 +448,9 @@
             vmem((rows, 2 * LANES), bf16),
             vmem((rows, 2 * LANES), bf16),
             *[vmem((rows, 2 * LANES), f32)] * 4,
-            vmem((n_dp, n_ctx // group, 8, LANES), f32),
-            vmem((n_dp - 1, n_ctx // group, 8, LANES), f32),
+            vmem((n_dp, n_ctx // n_dp, CHANS, LANES), f32),
+            vmem((n_dp, n_ctx // n_dp, CHANS, LANES), bf16),
+            vmem((n_dp - 1, n_ctx // n_dp, CHANS, LANES), bf16),
             dma((9,)),
             dma((2, n_tp // 2, CHUNKS)),
             dma((2, n_tp // 2, CHUNKS)),
@@ -466,7 +458,7 @@
             dma((4,)),
             dma((n_dp - 1,)),
             dma((n_dp - 1,)),
-            pltpu.SemaphoreType.REGULAR((n_ctx // 8 - 1 + n_dp + 1,)),
+            pltpu.SemaphoreType.REGULAR,
         ],
         compiler_params=pltpu.CompilerParams(
             collective_id=0, has_side_effects=True, vmem_limit_bytes=MAIN_VMEM
@@ -478,7 +470,7 @@
     grad, gate, filt = pl.pallas_call(
         hand_over,
         out_shape=tuple(jax.ShapeDtypeStruct(a.shape, a.dtype) for a in (grad, gate, filt)),
-        in_specs=[pl.BlockSpec(memory_space=pl.ANY)] * 3,
+        in_specs=[whole] * 3,
         out_specs=(pl.BlockSpec(memory_space=pltpu.HBM),) * 3,
         scratch_shapes=[dma((3,))],
         compiler_params=pltpu.CompilerParams(vmem_limit_bytes=FINISH_VMEM),

time: 69.2 us -> 57.4 us (0.83)
  Pallas kernels: 65.7 us -> 56.6 us
  local copies, waits for them, and re-layouts: 2.64 us -> 0 us
    pallas_call x1, Pallas kernels: 64.9 us -> 55.9 us  [on_device(): pl.pallas_call(functools.partial(kernel, n_ctx, n_tp, n_dp), out_shape=(v...]
    unnamed x6 -> x0, local copies, waits for them, and re-layouts: 2.64 us -> none
where the time goes in v3:
time: 57.4 us; the launch traced here: 57.3 us
  Pallas kernels  56.6 us (99%)
  between operations  0.64 us (1%)
    pallas_call x1, Pallas kernels, on_device(): pl.pallas_call(functools.partial(kernel, n_ctx, n_tp, n_dp), out_shape=(v...  55.9 us

profile of v3, /device:TPU:1, one launch (start us, length us, event | category | flops | bytes accessed | tf_op | source)
XLA Modules:
  0.0 57.3 jit_solution(12333879842398663515)
XLA Ops:
  0.6 55.9 %shard_map.112 = (bf16[512,128]{1,0:T(8,128)(2,1)S(1)}, bf16[512,128]{1,0:T(8,128)(2,1)S(1)}, f32[4,4096]{1,0:T(4,128)S(1)}) custom-call(bf16[16,4096]{1,0:T(8,128)(2,1)} %bitcast.5, bf16[512,128]{1,0:T(8,128)(2,1)} %bitcast.6, bf16[512,128]{1,0:T(8,128)(2,1)} %bitcast.7, f32[16,4096]{1,0:T(8,128)} %filt_hbm.1, bf16[512,4096]{1,0:T(8,128)(2,1)} %weight_hbm.1, ...), custom_call_target="tpu_custom_call" | custom-call | tf_op jit(solution)/shard_map/pallas_call | solution.py:427
  56.5 0.7 %shard_map.113 = (bf16[512,128]{1,0:T(8,128)(2,1)}, bf16[512,128]{1,0:T(8,128)(2,1)}, f32[4,4096]{1,0:T(4,128)}) custom-call(bf16[512,128]{1,0:T(8,128)(2,1)S(1)} %get-tuple-element.9.refs_0_, bf16[512,128]{1,0:T(8,128)(2,1)S(1)} %get-tuple-element.10.refs_1_, f32[4,4096]{1,0:T(4,128)S(1)} %get-tuple-element.11.refs_2_), custom_call_target="tpu_custom_call" | custom-call | tf_op jit(solution)/shard_map/pallas_call | solution.py:470

commit v4 on v3

--- a/solution.py
+++ b/solution.py
@@ -181,7 +181,7 @@
     ]
 
     barrier = pltpu.get_barrier_semaphore()
-    first = [{"tp": right}, {"tp": left}] + y_lines + z_line
+    first = y_lines + z_line + [{"tp": right}, {"tp": left}]
     for peer in first:
         pl.semaphore_signal(barrier, inc=1, device_id=peer, device_id_type=MESH)
 
@@ -197,6 +197,7 @@
     ]
     for load in loads:
         load.start()
+    loads[0].wait()
     pl.semaphore_wait(barrier, len(first))
 
     width = ring.shape[2] // CHUNKS
@@ -207,7 +208,7 @@
         cols = pl.ds(chunk * width, width)
         block = ring.at[origin, :, cols]
         return pltpu.make_async_remote_copy(
-            src_ref=block if step else grad_hbm.at[:, cols],
+            src_ref=block,
             dst_ref=block,
             send_sem=ring_send.at[way, step, chunk],
             recv_sem=ring_recv.at[way, step, chunk],
@@ -253,26 +254,34 @@
         [filt_buf[:, pl.ds(j * LANES, LANES)] for j in range(n_ctx)],
         twist, ahead, high, low, spec_filt,
     )
-    loads[0].wait()
     loads[1].wait()
 
     mine = pl.ds(pl.multiple_of(ctx * CHANS, CHANS), CHANS)
 
+    def give(which, source, target, peer):
+        theirs = pl.ds(pl.multiple_of(peer * CHANS, CHANS), CHANS)
+        pltpu.make_async_remote_copy(
+            src_ref=source.at[theirs, :],
+            dst_ref=target.at[mine, :],
+            send_sem=swap_send.at[which],
+            recv_sem=swap_recv.at[which],
+            device_id={"ctx": peer},
+            device_id_type=MESH,
+        ).start()
+
+    y_at, side = ctx // 4, lax.rem(ctx, 4)
+
     def exchange(which, source, target):
-        def send(i, carry):
-            peer = lax.rem(ctx + i, n_ctx)
-            theirs = pl.ds(pl.multiple_of(peer * CHANS, CHANS), CHANS)
-            pltpu.make_async_remote_copy(
-                src_ref=source.at[theirs, :],
-                dst_ref=target.at[mine, :],
-                send_sem=swap_send.at[which],
-                recv_sem=swap_recv.at[which],
-                device_id={"ctx": peer},
-                device_id_type=MESH,
-            ).start()
+        def send(a, carry):
+            ahead_by = n_y // 2 + (a + 1) // 2 * (1 - 2 * lax.rem(a, 2))
+            line = lax.rem(y_at + ahead_by, n_y) * 4
+            for turn in (2, 3, 1, 0):
+                give(which, source, target, line + lax.rem(side + turn, 4))
             return carry
 
-        lax.fori_loop(1, n_ctx, send, 0)
+        lax.fori_loop(0, n_y - 1, send, 0)
+        for turn in (2, 3, 1):
+            give(which, source, target, y_at * 4 + lax.rem(side + turn, 4))
         target[mine, :] = source[mine, :]
 
     def exchanged(which, source, target):
@@ -312,20 +321,27 @@
     loads[7].wait()
     loads[8].wait()
     tokens = ring[...].reshape(LANES, ring.shape[2])
-    tile = min(128, unit.shape[0])
-
-    def project(i, carry):
-        rows = pl.ds(pl.multiple_of(i * tile, tile), tile)
+    per_tile = 8
+    tile_rows = per_tile * CHANS
+    n_tiles = n_ctx // per_tile
+    my_tile, my_place = ctx // per_tile, lax.rem(ctx, per_tile)
+    for k in sorted(range(n_tiles), key=lambda k: -min(k, n_tiles - k)):
+        tile = lax.rem(my_tile + k, n_tiles)
+        rows = pl.ds(pl.multiple_of(tile * tile_rows, tile_rows), tile_rows)
         grad = lax.dot_general(
             weight[rows, :], tokens, (((1,), (1,)), ((), ())),
             preferred_element_type=jnp.float32,
         )
         unit[rows, :] = grad
         gate_send[rows, :] = (grad * gate_buf[rows, :].astype(jnp.float32)).astype(jnp.bfloat16)
-        return carry
-
-    lax.fori_loop(0, unit.shape[0] // tile, project, 0)
-    exchange(1, gate_send, gate_in)
+
+        def send_tile(r, carry, tile=tile, k=k):
+            place_at = r if k else lax.rem(my_place + r, per_tile)
+            give(1, gate_send, gate_in, tile * per_tile + place_at)
+            return carry
+
+        lax.fori_loop(0 if k else 1, per_tile, send_tile, 0)
+    gate_in[mine, :] = gate_send[mine, :]
 
     exchanged(0, conv_buf, conv_in).wait_recv()
     ahead_transform(token_blocks(conv_in), twist, ahead, high, low, spec_conv)

time: 57.4 us -> 57.2 us (level)
  no operation moved by 1% of the time
where the time goes in v4:
time: 57.2 us; the launch traced here: 57 us
  Pallas kernels  56.4 us (99%)
  between operations  0.64 us (1%)
    pallas_call x1, Pallas kernels, on_device(): pl.pallas_call(functools.partial(kernel, n_ctx, n_tp, n_dp), out_shape=(v...  55.6 us

profile of v4, /device:TPU:1, one launch (start us, length us, event | category | flops | bytes accessed | tf_op | source)
XLA Modules:
  0.0 57.0 jit_solution(3922038956814430811)
XLA Ops:
  0.6 55.6 %shard_map.112 = (bf16[512,128]{1,0:T(8,128)(2,1)S(1)}, bf16[512,128]{1,0:T(8,128)(2,1)S(1)}, f32[4,4096]{1,0:T(4,128)S(1)}) custom-call(bf16[16,4096]{1,0:T(8,128)(2,1)} %bitcast.5, bf16[512,128]{1,0:T(8,128)(2,1)} %bitcast.6, bf16[512,128]{1,0:T(8,128)(2,1)} %bitcast.7, f32[16,4096]{1,0:T(8,128)} %filt_hbm.1, bf16[512,4096]{1,0:T(8,128)(2,1)} %weight_hbm.1, ...), custom_call_target="tpu_custom_call" | custom-call | tf_op jit(solution)/shard_map/pallas_call | solution.py:443
  56.3 0.7 %shard_map.113 = (bf16[512,128]{1,0:T(8,128)(2,1)}, bf16[512,128]{1,0:T(8,128)(2,1)}, f32[4,4096]{1,0:T(4,128)}) custom-call(bf16[512,128]{1,0:T(8,128)(2,1)S(1)} %get-tuple-element.9.refs_0_, bf16[512,128]{1,0:T(8,128)(2,1)S(1)} %get-tuple-element.10.refs_1_, f32[4,4096]{1,0:T(4,128)S(1)} %get-tuple-element.11.refs_2_), custom_call_target="tpu_custom_call" | custom-call | tf_op jit(solution)/shard_map/pallas_call | solution.py:486

commit v5 on v4

--- a/solution.py
+++ b/solution.py
@@ -13,6 +13,7 @@
 LANES = 128
 CHANS = 16
 CHUNKS = 4
+HEARD_AT = [(0, 1), (1, 0), (1, 3), (2, 2)]
 FINISH_VMEM = 1024 * 1024
 MAIN_VMEM = 64000 * 1024
 
@@ -174,16 +175,34 @@
     def place(y_at, z_at, core_at):
         return {"ctx": y_at * 4 + z_at // n_dp * 2 + core_at, "dp": lax.rem(z_at, n_dp)}
 
-    z_line = [place(y, lax.rem(z + d, n_z), core) for d in range(1, n_z)]
-    y_lines = [
-        place(lax.rem(y + d, n_y), z, lax.rem(core + c, 2))
-        for d in range(n_y) for c in (0, 1) if d or c
-    ]
+    def offsets(size, *steps):
+        return sorted({d % size for step in steps for d in (step, -step)} - {0})
+
+    y_two = [place(lax.rem(y + d, n_y), z, core) for d in offsets(n_y, 2)]
+    z_two = [place(y, lax.rem(z + d, n_z), core) for d in offsets(n_z, 2)]
+    y_near = [place(lax.rem(y + d, n_y), z, core) for d in offsets(n_y, 1, 2)]
+    z_near = [place(y, lax.rem(z + d, n_z), core) for d in offsets(n_z, 1, 2)]
+    other_core = [place(y, z, 1 - core)]
 
     barrier = pltpu.get_barrier_semaphore()
-    first = y_lines + z_line + [{"tp": right}, {"tp": left}]
+    first = y_near + z_near + other_core + [{"tp": right}, {"tp": left}]
     for peer in first:
         pl.semaphore_signal(barrier, inc=1, device_id=peer, device_id_type=MESH)
+    rounds = [z_near]
+    if n_y > 4:
+        rounds.insert(0, y_two)
+    if n_z > 4:
+        rounds.append(z_two)
+    rounds.append(other_core)
+
+    def tell(at):
+        for peer in rounds[at]:
+            pl.semaphore_signal(news.at[at], inc=1, device_id=peer, device_id_type=MESH)
+
+    def hear(at):
+        pl.semaphore_wait(news.at[at], len(rounds[at]))
+        if at + 1 < len(rounds):
+            tell(at + 1)
 
     loads = [
         pltpu.make_async_copy(src, dst, load_sem.at[i])
@@ -244,8 +263,7 @@
     for turn in range(CHUNKS):
         for way in (0, 1):
             forward(way, 0, orders[way][turn])
-    for peer in z_line:
-        pl.semaphore_signal(news, inc=1, device_id=peer, device_id_type=MESH)
+    tell(0)
 
     loads[2].wait()
     loads[3].wait()
@@ -311,9 +329,11 @@
                 arrival(way, step, chunk).wait_recv()
                 if way in ways(step + 1, chunk):
                     forward(way, step + 1, chunk)
-            if step == 0 and turn == 1:
-                pl.semaphore_wait(news, len(z_line))
-                exchange(0, conv_buf, conv_in)
+            if (step, turn) in HEARD_AT[: len(rounds)]:
+                at = HEARD_AT.index((step, turn))
+                hear(at)
+                if at + 1 == len(rounds):
+                    exchange(0, conv_buf, conv_in)
     for turn in range(CHUNKS // 2):
         for way in (0, 1):
             arrival(way, last, orders[way][turn]).wait_recv()
@@ -474,7 +494,7 @@
             dma((4,)),
             dma((n_dp - 1,)),
             dma((n_dp - 1,)),
-            pltpu.SemaphoreType.REGULAR,
+            pltpu.SemaphoreType.REGULAR((len(HEARD_AT),)),
         ],
         compiler_params=pltpu.CompilerParams(
             collective_id=0, has_side_effects=True, vmem_limit_bytes=MAIN_VMEM

time: 57.2 us -> 57.5 us (level)
  no operation moved by 1% of the time
where the time goes in v5:
time: 57.5 us; the launch traced here: 57.4 us
  Pallas kernels  56.7 us (99%)
  between operations  0.64 us (1%)
    pallas_call x1, Pallas kernels, on_device(): pl.pallas_call(functools.partial(kernel, n_ctx, n_tp, n_dp), out_shape=(v...  56 us

profile of v5, /device:TPU:1, one launch (start us, length us, event | category | flops | bytes accessed | tf_op | source)
XLA Modules:
  0.0 57.4 jit_solution(1376710468828783256)
XLA Ops:
  0.6 56.0 %shard_map.112 = (bf16[512,128]{1,0:T(8,128)(2,1)S(1)}, bf16[512,128]{1,0:T(8,128)(2,1)S(1)}, f32[4,4096]{1,0:T(4,128)S(1)}) custom-call(bf16[16,4096]{1,0:T(8,128)(2,1)} %bitcast.5, bf16[512,128]{1,0:T(8,128)(2,1)} %bitcast.6, bf16[512,128]{1,0:T(8,128)(2,1)} %bitcast.7, f32[16,4096]{1,0:T(8,128)} %filt_hbm.1, bf16[512,4096]{1,0:T(8,128)(2,1)} %weight_hbm.1, ...), custom_call_target="tpu_custom_call" | custom-call | tf_op jit(solution)/shard_map/pallas_call | solution.py:463
  56.6 0.7 %shard_map.113 = (bf16[512,128]{1,0:T(8,128)(2,1)}, bf16[512,128]{1,0:T(8,128)(2,1)}, f32[4,4096]{1,0:T(4,128)}) custom-call(bf16[512,128]{1,0:T(8,128)(2,1)S(1)} %get-tuple-element.9.refs_0_, bf16[512,128]{1,0:T(8,128)(2,1)S(1)} %get-tuple-element.10.refs_1_, f32[4,4096]{1,0:T(4,128)S(1)} %get-tuple-element.11.refs_2_), custom_call_target="tpu_custom_call" | custom-call | tf_op jit(solution)/shard_map/pallas_call | solution.py:506
